TPU v7x, 32 devices: a whole 2x2x4 slice. The times are simulated.
32 devices in a mesh: region: 4 (over y, x), scen: 8 (over z, core).
Axes of the slice: x: 2, y: 2, z: 4, core: 2. Of those that a mesh axis runs over, the one named last changes fastest.
Arguments:
- start_state: float32 [4, 128, 24, 1024], P('region', 'scen'), may hold values from -6 to 6
- price: float32 [4, 128, 24, 1024], P('region', 'scen'), may hold values from -6 to 6
- demand: float32 [4, 128, 24, 1024], P('region', 'scen'), may hold values from 0.2 to 2
- sens: bfloat16 [4, 1024, 1024], P('region'), as said below
- gen_bus: int32 [4, 512], P('region'), may hold values from 0 to 1023
- gen_cap: float32 [4, 512], P('region'), may hold values from 0.5 to 3
- tie_index: int32 [4, 2, 512], P('region'), may hold values from 0 to 1023, as said below
- tie_len: int32 [4, 2], P('region'), may hold values from 128 to 512, as said below
Outputs:
- final_state: float32 [4, 128, 24, 1024], P('region', 'scen')
- plan: float32 [4, 24, 1024], P('region')
Inputs may be any that keep to these rules, and one draw needn't show every extreme that they name: `tie_index`: for each region the two rows together hold each of the 1024 bus numbers exactly once. tie_len[r, 1] equals tie_len[(r + 1) mod 4, 0]; some border has exactly 512 live slots. `sens`: each matrix has a positive diagonal between 0.5 and 2 and off-diagonal entries of order 1 / sqrt(1024).
All inputs are finite; a program needn't handle non-finite values.
Results may differ from a plain program's by a relative error of at most 0.00098.
Values sent between devices are 32-bit elements; how exact they have to be, the bound alone decides.
A program may use at most 64 MiB of HBM per device.

v0:
```python
import jax
import jax.numpy as jnp
from jax import lax
from jax.sharding import PartitionSpec as P

SWEEPS = 2
STEPS = 3


step_rate = 0.3
tie_weight = 1.0
day_weight = 0.5


def shifted(value, axis, by):
    size = lax.axis_size(axis)
    return lax.ppermute(value, axis, [(i, (i + by) % size) for i in range(size)])


def select_dot(left, right):
    return jnp.dot(left, right, precision=lax.Precision.HIGHEST, preferred_element_type=jnp.float32)


def tie_target(state, permuter, live, tie_dual):
    scens, hours, buses = state.shape
    slots = live.shape[1]
    blocks = select_dot(state.reshape(-1, buses), permuter).reshape(scens, hours, 2, slots)
    from_left = shifted(blocks[:, :, 1], "region", 1)
    from_right = shifted(blocks[:, :, 0], "region", -1)
    theirs = jnp.stack([from_left, from_right], axis=2)
    middle = 0.5 * (blocks + theirs)
    tie_dual = tie_dual + blocks - middle
    target_blocks = (middle - tie_dual) * live
    target = select_dot(target_blocks.reshape(-1, buses), permuter.T).reshape(state.shape)
    return (target, tie_dual)


def day_ahead(state, day_dual, total_scen):
    local_sum = jnp.sum(state + day_dual, axis=0)
    share = lax.psum_scatter(local_sum, "scen", scatter_dimension=1, tiled=True)
    plan = lax.all_gather(share / total_scen, "scen", axis=1, tiled=True)
    return (plan, day_dual + state - plan[None])


def descend(state, prices, lower, matrix, target, tie_mask, plan, day_dual, upper):
    buses = state.shape[-1]
    for repeat in range(STEPS):
        rounded = state.reshape(-1, buses).astype(jnp.bfloat16)
        slope = jnp.dot(rounded, matrix, preferred_element_type=jnp.float32).reshape(state.shape)
        slope = (
            slope
            + prices
            + tie_weight * tie_mask * (state - target)
            + day_weight * (state - plan + day_dual)
        )
        state = jnp.clip(state - step_rate * slope, lower, upper)
    return state


def body(start_state, price, demand, sens, gen_bus, gen_cap, tie_index, tie_len):
    state = start_state[0]
    prices = price[0]
    lower = -demand[0]
    matrix = sens[0]
    indices = tie_index[0]
    buses = state.shape[-1]
    slots = indices.shape[1]
    total_scen = state.shape[0] * lax.axis_size("scen")
    bus_ids = jnp.arange(buses, dtype=jnp.int32)
    permuter = (bus_ids[:, None] == indices.reshape(-1)[None, :]).astype(jnp.float32)
    live = (jnp.arange(slots, dtype=jnp.int32)[None, :] < tie_len[0][:, None]).astype(jnp.float32)
    tie_mask = select_dot(permuter, live.reshape(-1))
    gen_onehot = (gen_bus[0][:, None] == bus_ids[None, :]).astype(jnp.float32)
    upper = select_dot(gen_cap[0][None, :], gen_onehot)[0]
    tie_dual = jnp.zeros(state.shape[:2] + (2, slots), jnp.float32)
    day_dual = jnp.zeros_like(state)
    plan = jnp.zeros(state.shape[1:], jnp.float32)
    for sweep in range(SWEEPS):
        target, tie_dual = tie_target(state, permuter, live, tie_dual)
        plan, day_dual = day_ahead(state, day_dual, total_scen)
        state = descend(state, prices, lower, matrix, target, tie_mask, plan, day_dual, upper)
    return (state[None], plan[None])


def solution(mesh):
    in_specs = (
        P("region", "scen", None, None),
        P("region", "scen", None, None),
        P("region", "scen", None, None),
        P("region", None, None),
        P("region", None),
        P("region", None),
        P("region", None, None),
        P("region", None),
    )
    out_specs = (P("region", "scen", None, None), P("region", None, None))
    return jax.shard_map(body, mesh=mesh, in_specs=in_specs, out_specs=out_specs, check_vma=False)
```

profile of v0, /device:TPU:0, one launch (start us, length us, event | category | flops | bytes accessed | tf_op | source)
XLA Modules:
  0.0 159.0 jit_solution(4747214662604481811)
XLA Ops:
  7.2 0.0 copy-start
  7.2 0.0 reduce-scatter.3.cloned.1.call-start
  7.2 0.8 copy.31
  8.1 5.4 %fusion.83 = f32[384,1024]{1,0:T(8,128)} fusion(f32[384,1024]{1,0:T(8,128)} %bitcast.201, s32[1024]{0:T(1024)S(1)} %bitcast.229), kind=kOutput, calls=%fused_computation.83 | convolution fusion | flops 4832886784 | bytes 3149824 | tf_op jit(solution)/shard_map/dot_general | solution.py:21
  13.4 3.4 %reshape.89 = f32[16,24,2,512]{3,2,1,0:T(2,128)} reshape(f32[384,1024]{1,0:T(8,128)} %fusion.83) | data formatting | bytes 3145728 | tf_op jit(solution)/shard_map/reshape | solution.py:27
  16.9 3.6 %fusion.96 = (f32[16,24,1,512]{3,2,1,0:T(1,128)S(1)}, f32[16,24,1,512]{3,2,1,0:T(1,128)S(1)}) fusion(f32[16,24,2,512]{3,2,1,0:T(2,128)} %reshape.89), kind=kLoop, calls=%fused_computation.105 | loop fusion | bytes 3145728 | tf_op jit(solution)/shard_map/slice | solution.py:28
  20.5 0.9 copy.39
  21.4 3.0 %collective-permute-start = (f32[16,24,512]{2,1,0:T(8,128)}, f32[16,24,512]{2,1,0:T(8,128)S(1)}, u32[]{:S(2)}, u32[]{:S(2)}) collective-permute-start(f32[16,24,512]{2,1,0:T(8,128)} %bitcast.200), channel_id=1, source_target_pairs={{0,8},{8,16},{16,24},{24,0},{1,9},{9,17},{17,25},{25,1},{2,10},{10... | collective-permute-start | bytes 2359304 | tf_op jit(solution)/shard_map/ppermute | solution.py:17
  24.4 0.9 copy.38
  25.3 1.0 collective-permute-start.1
  26.3 2.1 %reduce_sum.18 = f32[24,1024]{1,0:T(8,128)} reduce(f32[1,16,24,1024]{3,2,1,0:T(8,128)} %param.8, f32[]{:T(128)} %constant.2.clone.1), dimensions={0,1}, to_apply=%region_0.0 | reduce | flops 368640 | bytes 1671172 | tf_op jit(solution)/shard_map/reduce_sum | solution.py:39
  28.4 0.0 reduce-scatter.3.cloned.1.call-update
  28.4 0.0 reduce-scatter.5.cloned.1.call-start
  28.5 0.0 copy-done.11
  28.5 0.1 broadcast_bitcast_fusion
  28.6 0.1 lt.45
  28.7 0.8 fusion.2
  29.5 0.0 copy-done.13
  29.5 0.0 copy-done.14
  29.5 0.8 fusion.27
  30.3 29.7 %reduce-scatter.3.cloned.1.call-done = f32[24,128]{1,0:T(8,128)} async-done(((f32[24,1024]{1,0:T(8,128)}), f32[24,128]{1,0:T(8,128)}) %reduce-scatter.3.cloned.1.call-update) | async-done | bytes 12304 | tf_op jit(solution)/shard_map/reduce_scatter | solution.py:40
  60.0 0.7 broadcast_multiply_fusion.1
  60.7 14.1 %all_gather.6 = f32[24,1024]{1,0:T(8,128)S(1)} all-gather(f32[24,128]{1,0:T(8,128)S(1)} %broadcast_multiply_fusion.1), channel_id=1, replica_groups=mesh['region'=4,'scen'=8] {'scen'}, dimensions={1}, use_global_device_ids=true | all-gather | bytes 110592 | tf_op jit(solution)/shard_map/all_gather | solution.py:41
  74.8 0.0 collective-permute-done
  74.8 0.0 collective-permute-done.1
  74.8 1.3 pad_maximum_fusion
  76.1 1.2 copy.19
  77.3 0.0 copy-start.8
  77.3 0.3 copy.34
  77.7 1.1 copy-done.8
  78.7 0.4 fusion.28
  79.1 0.0 copy-start.1
  79.1 0.0 copy-start.3
  79.1 0.0 copy-start.6
  79.1 2.9 %fusion.5 = f32[16,24,1024]{2,1,0:T(8,128)S(1)} fusion(f32[16,24,1024]{2,1,0:T(8,128)S(1)} %bitcast.208, s32[1024]{0:T(1024)S(1)} %bitcast.231), kind=kOutput, calls=%fused_computation.6 | convolution fusion | flops 4832886784 | bytes 3149824 | tf_op jit(solution)/shard_map/dot_general | solution.py:21
  82.1 0.0 copy-done
  82.1 0.0 copy-done.1
  82.1 0.0 copy-done.3
  82.1 1.4 fusion.38
  83.5 1.5 fusion.44
  85.0 0.0 copy-start.12
  85.0 3.4 %fusion.94 = (f32[24,1024]{1,0:T(8,128)}, f32[16,24,1024]{2,1,0:T(8,128)}, f32[16,24,1024]{2,1,0:T(8,128)S(1)}) fusion(f32[24,1024]{1,0:T(8,128)S(1)} %all_gather.6, f32[1,16,24,1024]{3,2,1,0:T(8,128)S(1)} %copy-done.6, f32[16,24,1024]{2,1,0:T(8,128)S(1)} %fusion.44, f32[16,24,1024]{2,1,0:T(8,128)S(1)} %fusion.5, f32[1024]{0:T(1024)S(1)} %bitcast.211, ...), kind=kOutput, calls=%fused_computation.104 | convolution fusion | flops 811966464 | bytes 13312000 | tf_op jit(solution)/shard_map/dot_general | solution.py:49
  88.4 3.2 %fusion.8 = f32[16,24,2,512]{3,1,2,0:T(8,128)S(1)} fusion(s32[2,512]{1,0:T(2,128)S(1)} %bitcast.228, f32[16,24,1024]{2,1,0:T(8,128)S(1)} %get-tuple-element.10), kind=kOutput, calls=%fused_computation.8 | convolution fusion | flops 4832886784 | bytes 3149824 | tf_op jit(solution)/shard_map/dot_general | solution.py:21
  91.6 1.5 slice_bitcast_fusion.1
  93.1 0.3 copy-done.7
  93.4 1.5 collective-permute-start.2
  94.9 1.5 collective-permute-start.3
  96.3 0.0 reduce-scatter.5.cloned.1.call-update
  96.4 0.1 compare_convert_fusion
  96.4 27.9 %reduce-scatter.5.cloned.1.call-done = f32[24,128]{1,0:T(8,128)} async-done(((f32[24,1024]{1,0:T(8,128)}), f32[24,128]{1,0:T(8,128)}) %reduce-scatter.5.cloned.1.call-update) | async-done | bytes 12304 | tf_op jit(solution)/shard_map/reduce_scatter | solution.py:40
  124.4 0.7 broadcast_multiply_fusion
  125.1 13.9 %all_gather.7 = f32[24,1024]{1,0:T(8,128)S(1)} all-gather(f32[24,128]{1,0:T(8,128)S(1)} %broadcast_multiply_fusion), channel_id=1, replica_groups=mesh['region'=4,'scen'=8] {'scen'}, dimensions={1}, use_global_device_ids=true | all-gather | bytes 110592 | tf_op jit(solution)/shard_map/all_gather | solution.py:41
  139.0 0.0 collective-permute-done.2
  139.0 0.0 collective-permute-done.3
  139.0 3.5 %fusion.30 = f32[16,2,3,8,512]{4,3,2,1,0:T(8,128)S(1)} fusion(f32[16,24,2,512]{3,1,2,0:T(8,128)} %copy-done.7, f32[16,24,1,512]{3,1,2,0:T(8,128)} %bitcast.28, f32[16,24,1,512]{3,1,2,0:T(8,128)} %bitcast.26, f32[16,24,2,512]{3,2,1,0:T(2,128)} %reshape.89, f32[2,512]{1,0:T(2,128)S(1)} %compare_convert_fusion, f32[16,24,1,512]{3,1,2,0:T(8,128)} %bitcast.17, ...), kind=kLoop, calls=%fused_computation.32 | loop fusion | flops 4325376 | bytes 7868416
  142.5 0.2 copy.30
  142.7 0.0 copy-start.2
  142.7 0.0 copy-start.4
  142.7 0.0 copy-start.5
  142.7 2.9 %fusion.3 = f32[16,24,1024]{2,1,0:T(8,128)S(1)} fusion(f32[16,24,1024]{2,1,0:T(8,128)S(1)} %bitcast.207, s32[1024]{0:T(1024)S(1)} %bitcast.232), kind=kOutput, calls=%fused_computation.5 | convolution fusion | flops 4832886784 | bytes 3149824 | tf_op jit(solution)/shard_map/dot_general | solution.py:21
  145.7 1.6 fusion.56
  147.2 1.6 fusion.62
  148.8 2.7 %fusion.69 = f32[1,16,24,1024]{3,2,1,0:T(8,128)} fusion(f32[16,24,1024]{2,1,0:T(8,128)S(1)} %fusion.62, f32[1,16,24,1024]{3,2,1,0:T(8,128)S(1)} %copy-done.2, f32[16,24,1024]{2,1,0:T(8,128)S(1)} %fusion.3, bf16[1,1024,1024]{2,1,0:T(8,128)(2,1)S(1)} %copy-done, f32[16,24,1024]{2,1,0:T(8,128)S(1)} %copy-done.5, f32[1,16,24,1024]{3,2,1,0:T(8,128)S(1)} %copy-done.4, ...), kind=kOutput, calls=%fused_computation.79 | convolution fusion | flops 811204608 | bytes 11640832 | tf_op jit(solution)/shard_map/dot_general | solution.py:49
  151.5 0.6 copy.41
  (18 shorter events, 0.1 us)
Async XLA Ops:
  7.2 74.9 %copy-start = (bf16[1,1024,1024]{2,1,0:T(8,128)(2,1)S(1)}, bf16[1,1024,1024]{2,1,0:T(8,128)(2,1)}, u32[]{:S(2)}) copy-start(bf16[1,1024,1024]{2,1,0:T(8,128)(2,1)} %param.11) | copy-start | bytes 6291460
  7.2 52.8 %reduce-scatter.3.cloned.1.call-start = ((), (), s32[]{:S(2)}) async-start(), calls=%async_computation.2 | async-start | bytes 110592 | tf_op jit(solution)/shard_map/reduce_scatter | solution.py:40
  21.4 53.4 %collective-permute-start = (f32[16,24,512]{2,1,0:T(8,128)}, f32[16,24,512]{2,1,0:T(8,128)S(1)}, u32[]{:S(2)}, u32[]{:S(2)}) collective-permute-start(f32[16,24,512]{2,1,0:T(8,128)} %bitcast.200), channel_id=1, source_target_pairs={{0,8},{8,16},{16,24},{24,0},{1,9},{9,17},{17,25},{25,1},{2,10},{10... | collective-permute-start | bytes 2359304 | tf_op jit(solution)/shard_map/ppermute | solution.py:17
  24.4 4.1 %copy-start.11 = (s32[1,2]{1,0:T(1,128)S(1)}, s32[1,2]{1,0:T(1,128)}, u32[]{:S(2)}) copy-start(s32[1,2]{1,0:T(1,128)} %param.15) | copy-start | bytes 28
  25.3 4.2 %copy-start.13 = (s32[1,512]{1,0:T(1,128)S(1)}, s32[1,512]{1,0:T(1,128)}, u32[]{:S(2)}) copy-start(s32[1,512]{1,0:T(1,128)} %param.12) | copy-start | bytes 6148
  25.3 4.2 %copy-start.14 = (f32[1,512]{1,0:T(1,128)S(1)}, f32[1,512]{1,0:T(1,128)}, u32[]{:S(2)}) copy-start(f32[1,512]{1,0:T(1,128)} %param.13) | copy-start | bytes 6148
  25.3 49.5 %collective-permute-start.1 = (f32[16,24,512]{2,1,0:T(8,128)}, f32[16,24,512]{2,1,0:T(8,128)}, u32[]{:S(2)}, u32[]{:S(2)}) collective-permute-start(f32[16,24,512]{2,1,0:T(8,128)} %bitcast.199), channel_id=1, source_target_pairs={{0,24},{8,0},{16,8},{24,16},{1,25},{9,1},{17,9},{25,17},{2,26},{10... | collective-permute-start | bytes 2359304 | tf_op jit(solution)/shard_map/ppermute | solution.py:17
  28.4 95.9 %reduce-scatter.5.cloned.1.call-start = ((), (), s32[]{:S(2)}) async-start(), calls=%async_computation.3 | async-start | bytes 110592 | tf_op jit(solution)/shard_map/reduce_scatter | solution.py:40
  77.3 1.4 copy-start.8
  79.1 3.0 %copy-start.1 = (f32[1,16,24,1024]{3,2,1,0:T(8,128)S(1)}, f32[1,16,24,1024]{3,2,1,0:T(8,128)}, u32[]{:S(2)}) copy-start(f32[1,16,24,1024]{3,2,1,0:T(8,128)} %param.9) | copy-start | bytes 4718596
  79.1 3.0 %copy-start.3 = (f32[1,16,24,1024]{3,2,1,0:T(8,128)S(1)}, f32[1,16,24,1024]{3,2,1,0:T(8,128)}, u32[]{:S(2)}) copy-start(f32[1,16,24,1024]{3,2,1,0:T(8,128)} %param.10) | copy-start | bytes 4718596
  79.1 3.0 %copy-start.6 = (f32[1,16,24,1024]{3,2,1,0:T(8,128)S(1)}, f32[1,16,24,1024]{3,2,1,0:T(8,128)}, u32[]{:S(2)}) copy-start(f32[1,16,24,1024]{3,2,1,0:T(8,128)} %param.8) | copy-start | bytes 4718596
  85.0 3.4 %copy-start.12 = (s32[1,2,512]{2,1,0:T(2,128)S(1)}, s32[1,2,512]{2,1,0:T(2,128)}, u32[]{:S(2)}) copy-start(s32[1,2,512]{2,1,0:T(2,128)} %param.14) | copy-start | bytes 12292
  88.4 3.2 %copy-start.9 = (f32[16,24,1024]{2,1,0:T(8,128)}, f32[16,24,1024]{2,1,0:T(8,128)S(1)}, u32[]{:S(2)}) copy-start(f32[16,24,1024]{2,1,0:T(8,128)S(1)} %get-tuple-element.10) | copy-start | bytes 4718596
  91.6 1.8 %copy-start.7 = (f32[16,24,2,512]{3,1,2,0:T(8,128)}, f32[16,24,2,512]{3,1,2,0:T(8,128)S(1)}, u32[]{:S(2)}) copy-start(f32[16,24,2,512]{3,1,2,0:T(8,128)S(1)} %fusion.8) | copy-start | bytes 4718596
  93.4 45.6 %collective-permute-start.2 = (f32[16,24,512]{2,1,0:T(8,128)}, f32[16,24,512]{2,1,0:T(8,128)}, u32[]{:S(2)}, u32[]{:S(2)}) collective-permute-start(f32[16,24,512]{2,1,0:T(8,128)} %get-tuple-element.4), channel_id=1, source_target_pairs={{0,8},{8,16},{16,24},{24,0},{1,9},{9,17},{17,25},{25,1},{2,10},{10... | collective-permute-start | bytes 2359304 | tf_op jit(solution)/shard_map/ppermute | solution.py:17
  94.9 44.1 %collective-permute-start.3 = (f32[16,24,512]{2,1,0:T(8,128)}, f32[16,24,512]{2,1,0:T(8,128)}, u32[]{:S(2)}, u32[]{:S(2)}) collective-permute-start(f32[16,24,512]{2,1,0:T(8,128)} %get-tuple-element.5), channel_id=1, source_target_pairs={{0,24},{8,0},{16,8},{24,16},{1,25},{9,1},{17,9},{25,17},{2,26},{10... | collective-permute-start | bytes 2359304 | tf_op jit(solution)/shard_map/ppermute | solution.py:17
  142.5 3.2 %copy-start.10 = (f32[16,24,1024]{2,1,0:T(8,128)S(1)}, f32[16,24,1024]{2,1,0:T(8,128)}, u32[]{:S(2)}) copy-start(f32[16,24,1024]{2,1,0:T(8,128)} %copy-done.9) | copy-start | bytes 4718596
  142.7 3.0 %copy-start.2 = (f32[1,16,24,1024]{3,2,1,0:T(8,128)S(1)}, f32[1,16,24,1024]{3,2,1,0:T(8,128)}, u32[]{:S(2)}) copy-start(f32[1,16,24,1024]{3,2,1,0:T(8,128)} %param.9) | copy-start | bytes 4718596
  142.7 3.0 %copy-start.4 = (f32[1,16,24,1024]{3,2,1,0:T(8,128)S(1)}, f32[1,16,24,1024]{3,2,1,0:T(8,128)}, u32[]{:S(2)}) copy-start(f32[1,16,24,1024]{3,2,1,0:T(8,128)} %param.10) | copy-start | bytes 4718596
  142.7 3.0 %copy-start.5 = (f32[16,24,1024]{2,1,0:T(8,128)S(1)}, f32[16,24,1024]{2,1,0:T(8,128)}, u32[]{:S(2)}) copy-start(f32[16,24,1024]{2,1,0:T(8,128)} %get-tuple-element.3) | copy-start | bytes 4718596
Sparse Core Ops, SparseCore 0:
  28.5 31.4 reduce-scatter.2
  96.5 27.8 reduce-scatter.4
where the time goes:
time: 159 us
  waiting for transfers between devices  57.7 us (36%)
  matrix products  28.1 us (18%)
  blocking collectives  28 us (18%)
  local copies, waits for them, and re-layouts  15.2 us (10%)
  between operations  14.3 us (9%)
  other arithmetic  8.78 us (6%)
  starting transfers between devices  6.93 us (4%)
    reduce_scatter x2, waiting for transfers between devices, day_ahead(): share = lax.psum_scatter(local_sum, 'scen', scatter_dimension=1, tiled=True)  57.7 us
    all_gather x2, blocking collectives, day_ahead(): plan = lax.all_gather(share / total_scen, 'scen', axis=1, tiled=True)  28 us
    dot_general x6, matrix products, select_dot(): jnp.dot(left, right, precision=lax.Precision.HIGHEST, preferred_element_t...  16 us
    dot_general x6, matrix products, descend(): jnp.dot(rounded, matrix, preferred_element_type=jnp.float32)  12.1 us
    ppermute x4, starting transfers between devices, shifted(): lax.ppermute(value, axis, [(i, (i + by) % size) for i in range(size)])  6.85 us
    unnamed x39, local copies, waits for them, and re-layouts  5.19 us
    slice x1, local copies, waits for them, and re-layouts, tie_target(): from_left = shifted(blocks[:, :, 1], 'region', 1)  3.58 us
    unnamed x1, other arithmetic  3.5 us
  transfers between devices with their start and end apart: 6, of which 2 were waited for; matrix products, arithmetic and copies ran while one was open for 4% of the time, Pallas kernels for 0%

commit v1 on v0

v1 whole, which is shorter than its diff:
```python
import functools
import jax
import jax.numpy as jnp
from jax import lax
from jax.experimental import pallas as pl
from jax.experimental.pallas import tpu as pltpu
from jax.sharding import PartitionSpec as P

SWEEPS = 2
STEPS = 3
SUB = 8
LANES = 128
TILE = 256


step_rate = 0.3
tie_weight = 1.0
day_weight = 0.5

MESH = pl.DeviceIdType.MESH


def kernel(
    total_scen, regions, peers,
    s0_hbm, price_hbm, demand_hbm, sens_hbm, gen_bus, gen_cap, tie_index, tie_len,
    out_hbm, plan_out,
    st, dd, pr, dm, mat, pick, place, mrow, arow, urow, split, rb, kk,
    snd, rcv, pbuf,
    in_sem, mat_sem, out_sem, send_sem, recv_sem, psend_sem, precv_sem,
):
    chunks, scens, _, buses = st.shape
    slots = tie_index.shape[1]
    rows = scens * SUB
    tiles = buses // TILE
    me = lax.axis_index("scen")
    reg = lax.axis_index("region")
    up = lax.rem(reg + 1, regions)
    down = lax.rem(reg + regions - 1, regions)

    def load(kind, source, target, c):
        return pltpu.make_async_copy(source.at[:, pl.ds(pl.multiple_of(c * SUB, SUB), SUB), :], target.at[c], in_sem.at[kind, c])

    for c in range(chunks):
        load(0, s0_hbm, st, c).start()

    barrier = pltpu.get_barrier_semaphore()
    for other in (up, down):
        pl.semaphore_signal(barrier, inc=1, device_id={"region": other}, device_id_type=MESH)
    for d in range(1, peers):
        pl.semaphore_signal(barrier, inc=1, device_id={"scen": lax.rem(me + d, peers)}, device_id_type=MESH)

    mat_copy = pltpu.make_async_copy(sens_hbm, mat, mat_sem)
    mat_copy.start()
    for c in range(chunks):
        load(1, price_hbm, pr, c).start()
        load(2, demand_hbm, dm, c).start()

    def one_hot(hit):
        return jnp.where(hit, 1.0, 0.0)

    for k in range(2):
        wanted = jnp.broadcast_to(tie_index[k:k + 1, :], (LANES, slots))
        for b in range(buses // LANES):
            ids = lax.broadcasted_iota(jnp.int32, (LANES, slots), 0) + b * LANES
            pick[b * LANES:(b + 1) * LANES, k * slots:(k + 1) * slots] = one_hot(ids == wanted).astype(jnp.bfloat16)

    pl.semaphore_wait(barrier, 2 + peers - 1)

    def tie_copy(u, k):
        return pltpu.make_async_remote_copy(
            src_ref=snd.at[u, k], dst_ref=rcv.at[u, 1 - k],
            send_sem=send_sem.at[u, k], recv_sem=recv_sem.at[u, 1 - k],
            device_id={"region": (down, up)[k]}, device_id_type=MESH,
        )

    def plan_copy(u, d):
        return pltpu.make_async_remote_copy(
            src_ref=pbuf.at[u, me], dst_ref=pbuf.at[u, me],
            send_sem=psend_sem.at[u, d], recv_sem=precv_sem.at[u, me],
            device_id={"scen": lax.rem(me + d, peers)}, device_id_type=MESH,
        )

    def plan_arrival(u, d):
        src = lax.rem(me + d, peers)
        return pltpu.make_async_remote_copy(
            src_ref=pbuf.at[u, src], dst_ref=pbuf.at[u, src],
            send_sem=psend_sem.at[u, d], recv_sem=precv_sem.at[u, src],
            device_id={"scen": src}, device_id_type=MESH,
        )

    def put_split(value, at, width):
        high = value.astype(jnp.bfloat16)
        split[:rows, at:at + width] = high
        split[rows:, at:at + width] = (value - high.astype(jnp.float32)).astype(jnp.bfloat16)

    def select(weights, n):
        both = jnp.dot(split[...], weights[:, n * TILE:(n + 1) * TILE], preferred_element_type=jnp.float32)
        return both[:rows] + both[rows:]

    def send_ties(u, c):
        for n in range(tiles):
            put_split(st[c, :, :, n * TILE:(n + 1) * TILE].reshape(rows, TILE), n * TILE, TILE)
        per_side = slots // TILE
        for n in range(tiles):
            k, at = n // per_side, n % per_side
            snd[u, k, :, at * TILE:(at + 1) * TILE] = select(pick, n)
            if at == per_side - 1:
                tie_copy(u, k).start()

    def send_plan(u):
        for d in range(1, peers):
            plan_copy(u, d).start()

    def start_chunk(c, carry):
        load(0, s0_hbm, st, c).wait()
        send_ties(c, c)
        pbuf[c, me] = jnp.sum(st[c], axis=0)
        send_plan(c)
        return carry

    lax.fori_loop(0, chunks, start_chunk, 0)

    for k in range(2):
        column = jnp.transpose(jnp.broadcast_to(tie_index[k:k + 1, :].astype(jnp.float32), (LANES, slots))).astype(jnp.int32)
        alive = lax.broadcasted_iota(jnp.int32, (slots, LANES), 0) < tie_len[0, k]
        for b in range(buses // LANES):
            ids = lax.broadcasted_iota(jnp.int32, (slots, LANES), 1) + b * LANES
            hot = one_hot((ids == column) & alive)
            place[k * slots:(k + 1) * slots, b * LANES:(b + 1) * LANES] = hot.astype(jnp.bfloat16)
            part = jnp.broadcast_to(jnp.sum(hot, axis=0, keepdims=True), (SUB, LANES))
            if k == 0:
                mrow[:, b * LANES:(b + 1) * LANES] = part
            else:
                mrow[:, b * LANES:(b + 1) * LANES] += part
    arow[...] = 1.0 - step_rate * (tie_weight * mrow[...] + day_weight)
    gens = gen_bus.shape[1]
    column = jnp.transpose(jnp.broadcast_to(gen_bus[...].astype(jnp.float32), (LANES, gens))).astype(jnp.int32)
    caps = jnp.transpose(jnp.broadcast_to(gen_cap[...], (LANES, gens)))
    for b in range(buses // LANES):
        ids = lax.broadcasted_iota(jnp.int32, (gens, LANES), 1) + b * LANES
        part = jnp.sum(jnp.where(ids == column, caps, 0.0), axis=0, keepdims=True)
        urow[:, b * LANES:(b + 1) * LANES] = jnp.broadcast_to(part, (SUB, LANES))
    mat_copy.wait()

    def receive(sweep, u, c):
        for d in range(1, peers):
            plan_arrival(u, d).wait_recv()
        plan = pbuf[u, 0]
        for src in range(1, peers):
            plan = plan + pbuf[u, src]
        plan = plan / total_scen
        if sweep == SWEEPS - 1:
            plan_out[c] = plan
        for k in range(2):
            tie_copy(u, 1 - k).wait_recv()
            put_split(rcv[u, k], k * slots, slots)
        for n in range(tiles):
            cols = slice(n * TILE, (n + 1) * TILE)
            theirs = select(place, n).reshape(scens, SUB, TILE)
            now = st[c, :, :, cols]
            day = plan[:, cols]
            base = pr[c, :, :, cols]
            if sweep == 0:
                dual = now - day
                dd[c, :, :, cols] = dual
                pr[c, :, :, cols] = base + (0.5 * tie_weight) * (mrow[:, cols] * now - theirs)
            else:
                dual = dd[c, :, :, cols] + now - day
            kk[:, :, cols] = step_rate * (base - tie_weight * theirs + day_weight * (dual - day))
            rb[0, :, cols] = now.reshape(rows, TILE).astype(jnp.bfloat16)

    def descend(c):
        for step in range(STEPS):
            for n in range(tiles):
                cols = slice(n * TILE, (n + 1) * TILE)
                slope = jnp.dot(rb[step % 2], mat[:, cols], preferred_element_type=jnp.float32).reshape(scens, SUB, TILE)
                new = arow[:, cols] * st[c, :, :, cols] - step_rate * slope - kk[:, :, cols]
                new = jnp.minimum(jnp.maximum(new, -dm[c, :, :, cols]), urow[:, cols])
                st[c, :, :, cols] = new
                if step < STEPS - 1:
                    rb[(step + 1) % 2, :, cols] = new.reshape(rows, TILE).astype(jnp.bfloat16)

    def first_sweep(c, carry):
        load(1, price_hbm, pr, c).wait()
        load(2, demand_hbm, dm, c).wait()
        receive(0, c, c)
        descend(c)
        send_ties(chunks + c, c)
        pbuf[chunks + c, me] = jnp.sum(st[c] + dd[c], axis=0)
        send_plan(chunks + c)
        return carry

    lax.fori_loop(0, chunks, first_sweep, 0)

    def store(c):
        return pltpu.make_async_copy(st.at[c], out_hbm.at[:, pl.ds(pl.multiple_of(c * SUB, SUB), SUB), :], out_sem.at[c])

    def last_sweep(c, carry):
        receive(1, chunks + c, c)
        descend(c)
        store(c).start()
        return carry

    lax.fori_loop(0, chunks, last_sweep, 0)

    def finish(u, carry):
        for k in range(2):
            tie_copy(u, k).wait_send()
        for d in range(1, peers):
            plan_copy(u, d).wait_send()
        return carry

    lax.fori_loop(0, SWEEPS * chunks, finish, 0)
    for c in range(chunks):
        store(c).wait()


def body(start_state, price, demand, sens, gen_bus, gen_cap, tie_index, tie_len):
    _, scens, hours, buses = start_state.shape
    slots = tie_index.shape[2]
    peers = lax.axis_size("scen")
    regions = lax.axis_size("region")
    chunks = hours // SUB
    rows = scens * SUB
    f32, bf16 = jnp.float32, jnp.bfloat16
    resident = pl.BlockSpec(memory_space=pltpu.VMEM)
    anywhere = pl.BlockSpec(memory_space=pl.ANY)
    whole = pltpu.VMEM((chunks, scens, SUB, buses), f32)
    final, plan = pl.pallas_call(
        functools.partial(kernel, scens * peers, regions, peers),
        out_shape=(
            jax.ShapeDtypeStruct((scens, hours, buses), f32),
            jax.ShapeDtypeStruct((chunks, SUB, buses), f32),
        ),
        in_specs=[anywhere] * 4 + [resident] * 3 + [pl.BlockSpec(memory_space=pltpu.SMEM)],
        out_specs=(anywhere, resident),
        scratch_shapes=[
            whole, whole, whole, whole,
            pltpu.VMEM((buses, buses), bf16),
            pltpu.VMEM((buses, 2 * slots), bf16),
            pltpu.VMEM((2 * slots, buses), bf16),
            pltpu.VMEM((SUB, buses), f32),
            pltpu.VMEM((SUB, buses), f32),
            pltpu.VMEM((SUB, buses), f32),
            pltpu.VMEM((2 * rows, buses), bf16),
            pltpu.VMEM((2, rows, buses), bf16),
            pltpu.VMEM((scens, SUB, buses), f32),
            pltpu.VMEM((SWEEPS * chunks, 2, rows, slots), f32),
            pltpu.VMEM((SWEEPS * chunks, 2, rows, slots), f32),
            pltpu.VMEM((SWEEPS * chunks, peers, SUB, buses), f32),
            pltpu.SemaphoreType.DMA((3, chunks)),
            pltpu.SemaphoreType.DMA,
            pltpu.SemaphoreType.DMA((chunks,)),
            pltpu.SemaphoreType.DMA((SWEEPS * chunks, 2)),
            pltpu.SemaphoreType.DMA((SWEEPS * chunks, 2)),
            pltpu.SemaphoreType.DMA((SWEEPS * chunks, peers)),
            pltpu.SemaphoreType.DMA((SWEEPS * chunks, peers)),
        ],
        compiler_params=pltpu.CompilerParams(collective_id=0, has_side_effects=True),
        name="dispatch",
    )(start_state[0], price[0], demand[0], sens[0], gen_bus, gen_cap, tie_index[0], tie_len)
    return (final[None], plan.reshape(1, hours, buses))


def solution(mesh):
    in_specs = (
        P("region", "scen", None, None),
        P("region", "scen", None, None),
        P("region", "scen", None, None),
        P("region", None, None),
        P("region", None),
        P("region", None),
        P("region", None, None),
        P("region", None),
    )
    out_specs = (P("region", "scen", None, None), P("region", None, None))
    return jax.shard_map(body, mesh=mesh, in_specs=in_specs, out_specs=out_specs, check_vma=False)
```

time: 159 us -> 86.1 us (0.54)
  Pallas kernels: 0 us -> 81.8 us
  waiting for transfers between devices: 57.7 us -> 0 us
  matrix products: 28.1 us -> 0 us
  blocking collectives: 28 us -> 0 us
  between operations: 14.3 us -> 0.65 us
  local copies, waits for them, and re-layouts: 15.2 us -> 3.41 us
  other arithmetic: 8.78 us -> 0 us
  starting transfers between devices: 6.93 us -> 0 us
    pallas_call x0 -> x1, Pallas kernels: none -> 81.8 us  [body(): pl.pallas_call(functools.partial(kernel, scens * peers, regions, peers),...]
    reduce_scatter x2 -> x0, waiting for transfers between devices: 57.7 us -> none  [day_ahead(): share = lax.psum_scatter(local_sum, 'scen', scatter_dimension=1, tiled=True)]
    dot_general x12 -> x0, matrix products: 28.1 us -> none  [the longest x6 16 us: select_dot(): jnp.dot(left, right, precision=lax.Precision.HIGHEST, preferred_element_t...]
    all_gather x2 -> x0, blocking collectives: 28 us -> none  [day_ahead(): plan = lax.all_gather(share / total_scen, 'scen', axis=1, tiled=True)]
    ppermute x4 -> x0, starting transfers between devices: 6.85 us -> none  [shifted(): lax.ppermute(value, axis, [(i, (i + by) % size) for i in range(size)])]
    slice x1 -> x0, local copies, waits for them, and re-layouts: 3.58 us -> none  [tie_target(): from_left = shifted(blocks[:, :, 1], 'region', 1)]
    unnamed x1 -> x0, other arithmetic: 3.5 us -> none
    reshape x1 -> x0, local copies, waits for them, and re-layouts: 3.44 us -> none  [tie_target(): select_dot(state.reshape(-1, buses), permuter)]
  transfers between devices with their start and end apart: 6 -> 0, of which waited for: 2 -> 0; matrix products, arithmetic and copies ran while one was open for 4% -> 0% of each run, Pallas kernels for 0% -> 0%
where the time goes in v1:
time: 86.1 us; the launch traced here: 85.9 us
  Pallas kernels  81.8 us (95%)
  local copies, waits for them, and re-layouts  3.41 us (4%)
    pallas_call x1, Pallas kernels, body(): pl.pallas_call(functools.partial(kernel, scens * peers, regions, peers),...  81.8 us
    unnamed x4, local copies, waits for them, and re-layouts  3.41 us

profile of v1, /device:TPU:0, one launch (start us, length us, event | category | flops | bytes accessed | tf_op | source)
XLA Modules:
  0.0 85.9 jit_solution(10759876862514024573)
XLA Ops:
  0.6 81.8 %dispatch.1 = (f32[16,24,1024]{2,1,0:T(8,128)}, f32[3,8,1024]{2,1,0:T(8,128)}) custom-call(f32[16,24,1024]{2,1,0:T(8,128)} %bitcast.9, f32[16,24,1024]{2,1,0:T(8,128)} %bitcast.10, f32[16,24,1024]{2,1,0:T(8,128)} %bitcast.11, bf16[1024,1024]{1,0:T(8,128)(2,1)} %bitcast.7, s32[1,512]{1,0:T(1,128)} %gen_bus.1, f32[1,512]{1,0:T(1,128)} %gen_cap.1, ...), custom_call_target="tpu_custom_call" | custom-call | tf_op jit(solution)/shard_map/dispatch/pallas_call | solution.py:229
  82.5 0.0 copy-start
  82.5 2.8 %copy.12 = f32[1,16,24,1024]{3,2,1,0:T(8,128)} copy(f32[1,16,24,1024]{3,2,1,0:T(8,128)} %bitcast.8) | data formatting | bytes 3145728
  85.2 0.0 copy-done
  85.2 0.6 copy.13
Async XLA Ops:
  82.5 2.8 %copy-start = (f32[3,8,1024]{2,1,0:T(8,128)S(1)}, f32[3,8,1024]{2,1,0:T(8,128)}, u32[]{:S(2)}) copy-start(f32[3,8,1024]{2,1,0:T(8,128)} %get-tuple-element.5) | copy-start | bytes 294916

commit v2 on v1

--- a/solution.py
+++ b/solution.py
@@ -11,6 +11,7 @@
 SUB = 8
 LANES = 128
 TILE = 256
+PARTS = 2
 
 
 step_rate = 0.3
@@ -23,10 +24,10 @@
 def kernel(
     total_scen, regions, peers,
     s0_hbm, price_hbm, demand_hbm, sens_hbm, gen_bus, gen_cap, tie_index, tie_len,
-    out_hbm, plan_out,
-    st, dd, pr, dm, mat, pick, place, mrow, arow, urow, split, rb, kk,
+    out, plan_out,
+    st, dd, pr, dm, mat, pick, place, mrow, arow, urow, split, rb, kk, first,
     snd, rcv, pbuf,
-    in_sem, mat_sem, out_sem, send_sem, recv_sem, psend_sem, precv_sem,
+    in_sem, mat_sem, send_sem, recv_sem, psend_sem, precv_sem,
 ):
     chunks, scens, _, buses = st.shape
     slots = tie_index.shape[1]
@@ -58,18 +59,20 @@
     def one_hot(hit):
         return jnp.where(hit, 1.0, 0.0)
 
-    for k in range(2):
+    def build_pick(k):
         wanted = jnp.broadcast_to(tie_index[k:k + 1, :], (LANES, slots))
         for b in range(buses // LANES):
             ids = lax.broadcasted_iota(jnp.int32, (LANES, slots), 0) + b * LANES
             pick[b * LANES:(b + 1) * LANES, k * slots:(k + 1) * slots] = one_hot(ids == wanted).astype(jnp.bfloat16)
 
+    build_pick(0)
     pl.semaphore_wait(barrier, 2 + peers - 1)
 
-    def tie_copy(u, k):
+    def tie_copy(u, k, part):
+        span = pl.ds(part * (rows // PARTS), rows // PARTS)
         return pltpu.make_async_remote_copy(
-            src_ref=snd.at[u, k], dst_ref=rcv.at[u, 1 - k],
-            send_sem=send_sem.at[u, k], recv_sem=recv_sem.at[u, 1 - k],
+            src_ref=snd.at[u, k, span], dst_ref=rcv.at[u, 1 - k, span],
+            send_sem=send_sem.at[u, k, part], recv_sem=recv_sem.at[u, 1 - k, part],
             device_id={"region": (down, up)[k]}, device_id_type=MESH,
         )
 
@@ -89,36 +92,47 @@
         )
 
     def put_split(value, at, width):
+        count = value.shape[0]
         high = value.astype(jnp.bfloat16)
-        split[:rows, at:at + width] = high
-        split[rows:, at:at + width] = (value - high.astype(jnp.float32)).astype(jnp.bfloat16)
-
-    def select(weights, n):
-        both = jnp.dot(split[...], weights[:, n * TILE:(n + 1) * TILE], preferred_element_type=jnp.float32)
-        return both[:rows] + both[rows:]
-
-    def send_ties(u, c):
+        split[:count, at:at + width] = high
+        split[count:2 * count, at:at + width] = (value - high.astype(jnp.float32)).astype(jnp.bfloat16)
+
+    def select(weights, n, count):
+        both = jnp.dot(split[:2 * count], weights[:, n * TILE:(n + 1) * TILE], preferred_element_type=jnp.float32)
+        return both[:count] + both[count:]
+
+    per_side = slots // TILE
+
+    def split_state(c):
         for n in range(tiles):
             put_split(st[c, :, :, n * TILE:(n + 1) * TILE].reshape(rows, TILE), n * TILE, TILE)
-        per_side = slots // TILE
-        for n in range(tiles):
-            k, at = n // per_side, n % per_side
-            snd[u, k, :, at * TILE:(at + 1) * TILE] = select(pick, n)
-            if at == per_side - 1:
-                tie_copy(u, k).start()
+
+    def gather_ties(u, k):
+        for at in range(per_side):
+            snd[u, k, :, at * TILE:(at + 1) * TILE] = select(pick, k * per_side + at, rows)
+
+    def send_ties(u, sides):
+        for part in range(PARTS):
+            for k in sides:
+                tie_copy(u, k, part).start()
 
     def send_plan(u):
         for d in range(1, peers):
             plan_copy(u, d).start()
 
-    def start_chunk(c, carry):
+    def start_chunk(c, peeled):
         load(0, s0_hbm, st, c).wait()
-        send_ties(c, c)
+        split_state(c)
+        for k in range(2):
+            if k == 1 and peeled:
+                build_pick(1)
+            gather_ties(c, k)
+            send_ties(c, (k,))
         pbuf[c, me] = jnp.sum(st[c], axis=0)
         send_plan(c)
-        return carry
-
-    lax.fori_loop(0, chunks, start_chunk, 0)
+
+    start_chunk(0, True)
+    pl.loop(1, chunks)(lambda c: start_chunk(c, False))
 
     for k in range(2):
         column = jnp.transpose(jnp.broadcast_to(tie_index[k:k + 1, :].astype(jnp.float32), (LANES, slots))).astype(jnp.int32)
@@ -142,7 +156,7 @@
         urow[:, b * LANES:(b + 1) * LANES] = jnp.broadcast_to(part, (SUB, LANES))
     mat_copy.wait()
 
-    def receive(sweep, u, c):
+    def prepare(sweep, u, c):
         for d in range(1, peers):
             plan_arrival(u, d).wait_recv()
         plan = pbuf[u, 0]
@@ -151,68 +165,91 @@
         plan = plan / total_scen
         if sweep == SWEEPS - 1:
             plan_out[c] = plan
-        for k in range(2):
-            tie_copy(u, 1 - k).wait_recv()
-            put_split(rcv[u, k], k * slots, slots)
         for n in range(tiles):
             cols = slice(n * TILE, (n + 1) * TILE)
-            theirs = select(place, n).reshape(scens, SUB, TILE)
             now = st[c, :, :, cols]
             day = plan[:, cols]
             base = pr[c, :, :, cols]
             if sweep == 0:
                 dual = now - day
                 dd[c, :, :, cols] = dual
-                pr[c, :, :, cols] = base + (0.5 * tie_weight) * (mrow[:, cols] * now - theirs)
+                pr[c, :, :, cols] = base + (0.5 * tie_weight) * mrow[:, cols] * now
             else:
                 dual = dd[c, :, :, cols] + now - day
-            kk[:, :, cols] = step_rate * (base - tie_weight * theirs + day_weight * (dual - day))
+            kk[:, :, cols] = step_rate * (base + day_weight * (dual - day))
             rb[0, :, cols] = now.reshape(rows, TILE).astype(jnp.bfloat16)
-
-    def descend(c):
-        for step in range(STEPS):
+        for n in range(tiles):
+            cols = slice(n * TILE, (n + 1) * TILE)
+            slope = jnp.dot(rb[0], mat[:, cols], preferred_element_type=jnp.float32).reshape(scens, SUB, TILE)
+            first[:, :, cols] = arow[:, cols] * st[c, :, :, cols] - step_rate * slope - kk[:, :, cols]
+
+    def descend(sweep, u, c, parts):
+        count = rows // PARTS * len(parts)
+        lines = slice(parts[0] * (rows // PARTS), parts[0] * (rows // PARTS) + count)
+        some = slice(lines.start // SUB, lines.stop // SUB)
+        for k in range(2):
+            for part in parts:
+                tie_copy(u, 1 - k, part).wait_recv()
+            put_split(rcv[u, k, lines], k * slots, slots)
+
+        def advance(n, new, step):
+            cols = slice(n * TILE, (n + 1) * TILE)
+            new = jnp.minimum(jnp.maximum(new, -dm[c, some, :, cols]), urow[:, cols])
+            if step < STEPS - 1:
+                rb[(step + 1) % 2, lines, cols] = new.reshape(count, TILE).astype(jnp.bfloat16)
+            if sweep == SWEEPS - 1 and step == STEPS - 1:
+                out[some, pl.ds(pl.multiple_of(c * SUB, SUB), SUB), cols] = new
+            else:
+                st[c, some, :, cols] = new
+
+        for n in range(tiles):
+            cols = slice(n * TILE, (n + 1) * TILE)
+            theirs = select(place, n, count).reshape(count // SUB, SUB, TILE)
+            if sweep == 0:
+                pr[c, some, :, cols] -= (0.5 * tie_weight) * theirs
+            pull = (step_rate * tie_weight) * theirs
+            kk[some, :, cols] -= pull
+            advance(n, first[some, :, cols] + pull, 0)
+        for step in range(1, STEPS):
             for n in range(tiles):
                 cols = slice(n * TILE, (n + 1) * TILE)
-                slope = jnp.dot(rb[step % 2], mat[:, cols], preferred_element_type=jnp.float32).reshape(scens, SUB, TILE)
-                new = arow[:, cols] * st[c, :, :, cols] - step_rate * slope - kk[:, :, cols]
-                new = jnp.minimum(jnp.maximum(new, -dm[c, :, :, cols]), urow[:, cols])
-                st[c, :, :, cols] = new
-                if step < STEPS - 1:
-                    rb[(step + 1) % 2, :, cols] = new.reshape(rows, TILE).astype(jnp.bfloat16)
-
-    def first_sweep(c, carry):
+                slope = jnp.dot(rb[step % 2, lines], mat[:, cols], preferred_element_type=jnp.float32).reshape(count // SUB, SUB, TILE)
+                advance(n, arow[:, cols] * st[c, some, :, cols] - step_rate * slope - kk[some, :, cols], step)
+
+    every = tuple(range(PARTS))
+
+    @pl.loop(0, chunks)
+    def first_sweep(c):
         load(1, price_hbm, pr, c).wait()
         load(2, demand_hbm, dm, c).wait()
-        receive(0, c, c)
-        descend(c)
-        send_ties(chunks + c, c)
-        pbuf[chunks + c, me] = jnp.sum(st[c] + dd[c], axis=0)
-        send_plan(chunks + c)
-        return carry
-
-    lax.fori_loop(0, chunks, first_sweep, 0)
-
-    def store(c):
-        return pltpu.make_async_copy(st.at[c], out_hbm.at[:, pl.ds(pl.multiple_of(c * SUB, SUB), SUB), :], out_sem.at[c])
-
-    def last_sweep(c, carry):
-        receive(1, chunks + c, c)
-        descend(c)
-        store(c).start()
-        return carry
-
-    lax.fori_loop(0, chunks, last_sweep, 0)
+        prepare(0, c, c)
+        descend(0, c, c, every)
+        u = chunks + c
+        pbuf[u, me] = jnp.sum(st[c] + dd[c], axis=0)
+        send_plan(u)
+        split_state(c)
+        for k in range(2):
+            gather_ties(u, k)
+        send_ties(u, (0, 1))
+
+    @pl.loop(0, chunks - 1)
+    def last_sweep(c):
+        prepare(1, chunks + c, c)
+        descend(1, chunks + c, c, every)
+
+    prepare(1, 2 * chunks - 1, chunks - 1)
+    for part in every:
+        descend(1, 2 * chunks - 1, chunks - 1, (part,))
 
     def finish(u, carry):
         for k in range(2):
-            tie_copy(u, k).wait_send()
+            for part in every:
+                tie_copy(u, k, part).wait_send()
         for d in range(1, peers):
             plan_copy(u, d).wait_send()
         return carry
 
     lax.fori_loop(0, SWEEPS * chunks, finish, 0)
-    for c in range(chunks):
-        store(c).wait()
 
 
 def body(start_state, price, demand, sens, gen_bus, gen_cap, tie_index, tie_len):
@@ -229,11 +266,11 @@
     final, plan = pl.pallas_call(
         functools.partial(kernel, scens * peers, regions, peers),
         out_shape=(
-            jax.ShapeDtypeStruct((scens, hours, buses), f32),
-            jax.ShapeDtypeStruct((chunks, SUB, buses), f32),
+            pltpu.VMEM((scens, hours, buses), f32),
+            pltpu.VMEM((chunks, SUB, buses), f32),
         ),
         in_specs=[anywhere] * 4 + [resident] * 3 + [pl.BlockSpec(memory_space=pltpu.SMEM)],
-        out_specs=(anywhere, resident),
+        out_specs=(resident, resident),
         scratch_shapes=[
             whole, whole, whole, whole,
             pltpu.VMEM((buses, buses), bf16),
@@ -245,14 +282,14 @@
             pltpu.VMEM((2 * rows, buses), bf16),
             pltpu.VMEM((2, rows, buses), bf16),
             pltpu.VMEM((scens, SUB, buses), f32),
+            pltpu.VMEM((scens, SUB, buses), f32),
             pltpu.VMEM((SWEEPS * chunks, 2, rows, slots), f32),
             pltpu.VMEM((SWEEPS * chunks, 2, rows, slots), f32),
             pltpu.VMEM((SWEEPS * chunks, peers, SUB, buses), f32),
             pltpu.SemaphoreType.DMA((3, chunks)),
             pltpu.SemaphoreType.DMA,
-            pltpu.SemaphoreType.DMA((chunks,)),
-            pltpu.SemaphoreType.DMA((SWEEPS * chunks, 2)),
-            pltpu.SemaphoreType.DMA((SWEEPS * chunks, 2)),
+            pltpu.SemaphoreType.DMA((SWEEPS * chunks, 2, PARTS)),
+            pltpu.SemaphoreType.DMA((SWEEPS * chunks, 2, PARTS)),
             pltpu.SemaphoreType.DMA((SWEEPS * chunks, peers)),
             pltpu.SemaphoreType.DMA((SWEEPS * chunks, peers)),
         ],

time: 86.1 us -> 82.6 us (0.959)
  Pallas kernels: 81.8 us -> 80 us
  local copies, waits for them, and re-layouts: 3.41 us -> 1.79 us
    pallas_call x1, Pallas kernels: 81.8 us -> 80 us  [body(): pl.pallas_call(functools.partial(kernel, scens * peers, regions, peers),...]
    unnamed x4 -> x2, local copies, waits for them, and re-layouts: 3.41 us -> 1.79 us
where the time goes in v2:
time: 82.6 us; the launch traced here: 82.4 us
  Pallas kernels  80 us (97%)
  local copies, waits for them, and re-layouts  1.79 us (2%)
    pallas_call x1, Pallas kernels, body(): pl.pallas_call(functools.partial(kernel, scens * peers, regions, peers),...  80 us
    unnamed x2, local copies, waits for them, and re-layouts  1.79 us

profile of v2, /device:TPU:0, one launch (start us, length us, event | category | flops | bytes accessed | tf_op | source)
XLA Modules:
  0.0 82.4 jit_solution(6454671905380932508)
XLA Ops:
  0.6 80.0 %dispatch.1 = (f32[16,24,1024]{2,1,0:T(8,128)S(1)}, f32[3,8,1024]{2,1,0:T(8,128)S(1)}) custom-call(f32[16,24,1024]{2,1,0:T(8,128)} %bitcast.10, f32[16,24,1024]{2,1,0:T(8,128)} %bitcast.11, f32[16,24,1024]{2,1,0:T(8,128)} %bitcast.12, bf16[1024,1024]{1,0:T(8,128)(2,1)} %bitcast.9, s32[1,512]{1,0:T(1,128)} %gen_bus.1, f32[1,512]{1,0:T(1,128)} %gen_cap.1, ...), custom_call_target="tpu_custom_call" | custom-call | tf_op jit(solution)/shard_map/dispatch/pallas_call | solution.py:266
  80.6 1.1 %copy.12 = f32[1,16,24,1024]{3,2,1,0:T(8,128)} copy(f32[1,16,24,1024]{3,2,1,0:T(8,128)S(1)} %bitcast.7) | data formatting | bytes 3145728
  81.8 0.6 copy.13

commit v3 on v2

--- a/solution.py
+++ b/solution.py
@@ -27,7 +27,7 @@
     out, plan_out,
     st, dd, pr, dm, mat, pick, place, mrow, arow, urow, split, rb, kk, first,
     snd, rcv, pbuf,
-    in_sem, mat_sem, send_sem, recv_sem, psend_sem, precv_sem,
+    token, in_sem, mat_sem, send_sem, recv_sem, psend_sem, precv_sem,
 ):
     chunks, scens, _, buses = st.shape
     slots = tie_index.shape[1]
@@ -47,8 +47,20 @@
     barrier = pltpu.get_barrier_semaphore()
     for other in (up, down):
         pl.semaphore_signal(barrier, inc=1, device_id={"region": other}, device_id_type=MESH)
-    for d in range(1, peers):
-        pl.semaphore_signal(barrier, inc=1, device_id={"scen": lax.rem(me + d, peers)}, device_id_type=MESH)
+    half = lax.rem(me, 2)
+    place_z = lax.div(me, 2)
+    last_z = peers // 2 - 1
+    lower, higher = {"scen": me - 2}, {"scen": me + 2}
+    pl.semaphore_signal(barrier, inc=1, device_id={"scen": me + 1 - 2 * half}, device_id_type=MESH)
+
+    @pl.when(place_z > 0)
+    def _():
+        pl.semaphore_signal(barrier, inc=1, device_id=lower, device_id_type=MESH)
+
+    @pl.when(place_z < last_z)
+    def _():
+        pl.semaphore_signal(barrier, inc=1, device_id=higher, device_id_type=MESH)
+
 
     mat_copy = pltpu.make_async_copy(sens_hbm, mat, mat_sem)
     mat_copy.start()
@@ -66,8 +78,6 @@
             pick[b * LANES:(b + 1) * LANES, k * slots:(k + 1) * slots] = one_hot(ids == wanted).astype(jnp.bfloat16)
 
     build_pick(0)
-    pl.semaphore_wait(barrier, 2 + peers - 1)
-
     def tie_copy(u, k, part):
         span = pl.ds(part * (rows // PARTS), rows // PARTS)
         return pltpu.make_async_remote_copy(
@@ -120,6 +130,27 @@
         for d in range(1, peers):
             plan_copy(u, d).start()
 
+    def enter():
+        pl.semaphore_wait(barrier, 3 + lax.div(place_z + last_z, last_z + 1) + lax.div(2 * last_z - place_z, last_z + 1))
+
+    def greet_far():
+        @pl.when(place_z == last_z)
+        def _():
+            pl.semaphore_signal(token.at[1], inc=1, device_id=lower, device_id_type=MESH)
+
+        @pl.when(place_z > 0)
+        def _():
+            pl.semaphore_wait(token.at[0], 1)
+
+        @pl.when(place_z < last_z)
+        def _():
+            pl.semaphore_signal(token.at[0], inc=1, device_id=higher, device_id_type=MESH)
+            pl.semaphore_wait(token.at[1], 1)
+
+        @pl.when((place_z > 0) & (place_z < last_z))
+        def _():
+            pl.semaphore_signal(token.at[1], inc=1, device_id=lower, device_id_type=MESH)
+
     def start_chunk(c, peeled):
         load(0, s0_hbm, st, c).wait()
         split_state(c)
@@ -127,9 +158,10 @@
             if k == 1 and peeled:
                 build_pick(1)
             gather_ties(c, k)
+            if k == 0 and peeled:
+                enter()
             send_ties(c, (k,))
         pbuf[c, me] = jnp.sum(st[c], axis=0)
-        send_plan(c)
 
     start_chunk(0, True)
     pl.loop(1, chunks)(lambda c: start_chunk(c, False))
@@ -154,6 +186,8 @@
         ids = lax.broadcasted_iota(jnp.int32, (gens, LANES), 1) + b * LANES
         part = jnp.sum(jnp.where(ids == column, caps, 0.0), axis=0, keepdims=True)
         urow[:, b * LANES:(b + 1) * LANES] = jnp.broadcast_to(part, (SUB, LANES))
+    greet_far()
+    pl.loop(0, chunks)(send_plan)
     mat_copy.wait()
 
     def prepare(sweep, u, c):
@@ -286,6 +320,7 @@
             pltpu.VMEM((SWEEPS * chunks, 2, rows, slots), f32),
             pltpu.VMEM((SWEEPS * chunks, 2, rows, slots), f32),
             pltpu.VMEM((SWEEPS * chunks, peers, SUB, buses), f32),
+            pltpu.SemaphoreType.REGULAR((2,)),
             pltpu.SemaphoreType.DMA((3, chunks)),
             pltpu.SemaphoreType.DMA,
             pltpu.SemaphoreType.DMA((SWEEPS * chunks, 2, PARTS)),

time: 82.6 us -> 79.7 us (0.965)
  Pallas kernels: 80 us -> 77.1 us
    pallas_call x1, Pallas kernels: 80 us -> 77.1 us  [body(): pl.pallas_call(functools.partial(kernel, scens * peers, regions, peers),...]
where the time goes in v3:
time: 79.7 us; the launch traced here: 79.5 us
  Pallas kernels  77.1 us (97%)
  local copies, waits for them, and re-layouts  1.79 us (2%)
    pallas_call x1, Pallas kernels, body(): pl.pallas_call(functools.partial(kernel, scens * peers, regions, peers),...  77.1 us
    unnamed x2, local copies, waits for them, and re-layouts  1.79 us

profile of v3, /device:TPU:0, one launch (start us, length us, event | category | flops | bytes accessed | tf_op | source)
XLA Modules:
  0.0 79.5 jit_solution(7922515071381783557)
XLA Ops:
  0.6 77.1 %dispatch.1 = (f32[16,24,1024]{2,1,0:T(8,128)S(1)}, f32[3,8,1024]{2,1,0:T(8,128)S(1)}) custom-call(f32[16,24,1024]{2,1,0:T(8,128)} %bitcast.10, f32[16,24,1024]{2,1,0:T(8,128)} %bitcast.11, f32[16,24,1024]{2,1,0:T(8,128)} %bitcast.12, bf16[1024,1024]{1,0:T(8,128)(2,1)} %bitcast.9, s32[1,512]{1,0:T(1,128)} %gen_bus.1, f32[1,512]{1,0:T(1,128)} %gen_cap.1, ...), custom_call_target="tpu_custom_call" | custom-call | tf_op jit(solution)/shard_map/dispatch/pallas_call | solution.py:300
  77.7 1.1 %copy.12 = f32[1,16,24,1024]{3,2,1,0:T(8,128)} copy(f32[1,16,24,1024]{3,2,1,0:T(8,128)S(1)} %bitcast.7) | data formatting | bytes 3145728
  78.9 0.6 copy.13
